TPU v7x, 256 devices: a whole 4x4x8 slice. The times are simulated.
256 devices in a mesh: rows: 32 (over z_lo, y, x), cols: 8 (over z_hi, core).
Axes of the slice: x: 4, y: 4, z: 8 (z_hi: 4, z_lo: 2; z = z_hi * 2 + z_lo), core: 2. Of those that a mesh axis runs over, the one named last changes fastest.
Arguments:
- canvas: bfloat16 [256, 1024, 256], P('rows', 'cols'), may hold values from -16 to 16
- conv_weight: bfloat16 [3, 3, 256, 512], replicated, may hold values from -0.125 to 0.125
- conv_bias: bfloat16 [512], replicated, may hold values from -3 to 3
- target_gram: float32 [512, 512], P(('rows', 'cols')), may hold values from -6 to 6
Outputs:
- gram: float32 [512, 512], P(('rows', 'cols'))
- grad_canvas: bfloat16 [256, 1024, 256], P('rows', 'cols')
All inputs are finite; a program needn't handle non-finite values.
Results may differ from a plain program's by a relative error of at most 0.009.
Values may be sent and summed in bfloat16 or wider, within the bound.
A program may use at most 64 MiB of HBM per device.

v0:
```python
import math

import jax
import jax.numpy as jnp
from jax import lax
from jax.sharding import PartitionSpec as P

gelu_scale = math.sqrt(2.0 / math.pi)


def padded_2(block, sides, width):
    for axis, dim in sides:
        count = lax.axis_size(axis)
        forward = [(i, i + 1) for i in range(count - 1)]
        backward = [(target, source) for source, target in forward]
        low = lax.ppermute(
            lax.slice_in_dim(block, block.shape[dim] - width, None, axis=dim), axis, forward
        )
        high = lax.ppermute(lax.slice_in_dim(block, 0, width, axis=dim), axis, backward)
        block = jnp.concatenate([low, block, high], axis=dim)
    return block


def gelu_grad(value):
    tangent = jnp.tanh(gelu_scale * (value + 0.044715 * value * value * value))
    return 0.5 * (1.0 + tangent) + 0.5 * value * (1.0 - tangent * tangent) * gelu_scale * (
        1.0 + 3.0 * 0.044715 * value * value
    )


def patches(padded, tile_rows, tile_cols):
    pieces = [
        padded[row_off : row_off + tile_rows, col_off : col_off + tile_cols, :]
        for row_off in range(3)
        for col_off in range(3)
    ]
    return jnp.concatenate(pieces, axis=2).reshape(tile_rows * tile_cols, -1)


def on_device(canvas, conv_weight, conv_bias, target_gram):
    tile_rows, tile_cols, in_width = canvas.shape
    out_width = conv_weight.shape[3]
    pixel_total = tile_rows * tile_cols * lax.axis_size("rows") * lax.axis_size("cols")
    padded = padded_2(canvas, (("rows", 0), ("cols", 1)), 1)
    kernel = conv_weight.reshape(9 * in_width, out_width)
    preact = jnp.dot(
        patches(padded, tile_rows, tile_cols), kernel, preferred_element_type=jnp.float32
    ) + conv_bias.astype(jnp.float32)
    features = jax.nn.gelu(preact, approximate=True).astype(jnp.bfloat16)
    gram_own = (
        lax.psum_scatter(
            lax.dot_general(
                features, features, (((0,), (0,)), ((), ())), preferred_element_type=jnp.float32
            ),
            ("rows", "cols"),
            scatter_dimension=0,
            tiled=True,
        )
        / pixel_total
    )
    error_own = gram_own - target_gram
    error_full = lax.all_gather(error_own, ("rows", "cols"), axis=0, tiled=True)
    symmetric = (error_full + error_full.T).astype(jnp.bfloat16)
    upstream = jnp.dot(features, symmetric, preferred_element_type=jnp.float32) / math.sqrt(
        out_width
    )
    grad_pre = (
        (upstream * gelu_grad(preact)).astype(jnp.bfloat16).reshape(tile_rows, tile_cols, out_width)
    )
    grad_padded = padded_2(grad_pre, (("rows", 0), ("cols", 1)), 1)
    flipped = conv_weight[::-1, ::-1].transpose(0, 1, 3, 2).reshape(9 * out_width, in_width)
    grad_canvas = jnp.dot(
        patches(grad_padded, tile_rows, tile_cols), flipped, preferred_element_type=jnp.float32
    )
    return (gram_own, grad_canvas.astype(jnp.bfloat16).reshape(tile_rows, tile_cols, in_width))


def solution(mesh):
    return jax.shard_map(
        on_device,
        mesh=mesh,
        in_specs=(P("rows", "cols", None), P(), P(), P(("rows", "cols"), None)),
        out_specs=(P(("rows", "cols"), None), P("rows", "cols", None)),
        check_vma=False,
    )
```

profile of v0, /device:TPU:1, one launch (start us, length us, event | category | flops | bytes accessed | tf_op | source)
XLA Modules:
  0.0 720.2 jit_solution(6664298643092920723)
XLA Ops:
  8.2 3.9 collective-permute-start
  12.1 1.3 collective-permute-start.1
  14.5 2.6 collective-permute-done.1
  17.2 6.9 collective-permute-start.2
  24.7 1.9 collective-permute-start.3
  26.9 3.8 collective-permute-done.3
  31.4 1.2 copy-done.1
  32.6 2.6 fusion.44
  35.2 1.3 copy-done.4
  36.5 2.8 fusion.30
  39.4 258.3 %all-reduce.3.cloned.1.call-done = f32[512,512]{1,0:T(8,128)} async-done(((f32[512,512]{1,0:T(8,128)}), f32[512,512]{1,0:T(8,128)}) %all-reduce.3.cloned.1.call-update) | async-done | bytes 1048592
  297.7 1.3 subtract_bitcast_fusion
  299.0 380.1 %all-gather.3.cloned.1.call-done = f32[256,2,512]{2,1,0:T(2,128)} async-done(((f32[1,2,512]{2,1,0:T(2,128)}), f32[256,2,512]{2,1,0:T(2,128)}) %all-gather.3.cloned.1.call-update) | async-done | bytes 1048592 | tf_op jit(solution)/shard_map/all_gather | solution.py:62
  679.1 1.9 reshape.39
  681.4 4.5 fusion.14
  686.6 1.3 collective-permute-start.5
  687.9 4.6 collective-permute-start.4
  692.6 2.8 copy.10
  695.4 1.6 rev.3
  697.8 2.7 collective-permute-start.7
  700.5 3.7 collective-permute-start.6
  705.4 1.6 pad_maximum_fusion
  708.5 1.5 copy-done.2
  710.0 3.4 convolution_convert_fusion
  (46 shorter events, 8.1 us)
Async XLA Ops:
  7.2 19.6 %copy-start = (bf16[8,128,256]{2,1,0:T(8,128)(2,1)S(1)}, bf16[8,128,256]{2,1,0:T(8,128)(2,1)}, u32[]{:S(2)}) copy-start(bf16[8,128,256]{2,1,0:T(8,128)(2,1)} %param.4) | copy-start | bytes 1572868
  7.2 290.5 %all-reduce.3.cloned.1.call-start = ((), (), s32[]{:S(2)}) async-start(), calls=%async_computation.1 | async-start | bytes 2097152
  8.2 5.3 collective-permute-start
  12.1 5.0 collective-permute-start.1
  17.2 9.5 %collective-permute-start.2 = (bf16[10,1,256]{2,1,0:T(2,128)(2,1)S(1)}, bf16[10,1,256]{2,1,0:T(2,128)(2,1)S(1)}, u32[]{:S(2)}, u32[]{:S(2)}) collective-permute-start(bf16[10,1,256]{2,1,0:T(2,128)(2,1)S(1)} %get-tuple-element.19), channel_id=1, source_target_pairs={{0,1},{1,2},{2,3},{3,4},{4,5},{5,6},{6,7},{8,9},{9,10},{10,11},{11... | collective-permute-start | bytes 15368 | tf_op jit(solution)/shard_map/ppermute | solution.py:16
  24.7 5.9 collective-permute-start.3
  30.9 1.7 copy-start.1
  35.2 1.3 copy-start.4
  36.5 261.1 %copy-start.3 = (f32[2,512]{1,0:T(2,128)S(1)}, f32[2,512]{1,0:T(2,128)}, u32[]{:S(2)}) copy-start(f32[2,512]{1,0:T(2,128)} %param.7) | copy-start | bytes 12292
  39.3 639.8 %all-gather.3.cloned.1.call-start = ((), (), s32[]{:S(2)}) async-start(), calls=%async_computation | async-start | bytes 1052672 | tf_op jit(solution)/shard_map/all_gather | solution.py:62
  686.6 10.4 %collective-permute-start.5 = (bf16[1,128,512]{2,1,0:T(8,128)(2,1)}, bf16[1,128,512]{2,1,0:T(8,128)(2,1)S(1)}, u32[]{:S(2)}, u32[]{:S(2)}) collective-permute-start(bf16[1,128,512]{2,1,0:T(8,128)(2,1)} %get-tuple-element.17), channel_id=1, source_target_pairs={{8,0},{16,8},{24,16},{32,24},{40,32},{48,40},{56,48},{64,56},{72,6... | collective-permute-start | bytes 393224 | tf_op jit(solution)/shard_map/ppermute | solution.py:19
  687.9 9.1 %collective-permute-start.4 = (bf16[1,128,512]{2,1,0:T(8,128)(2,1)}, bf16[1,128,512]{2,1,0:T(8,128)(2,1)}, u32[]{:S(2)}, u32[]{:S(2)}) collective-permute-start(bf16[1,128,512]{2,1,0:T(8,128)(2,1)} %get-tuple-element.16), channel_id=1, source_target_pairs={{0,8},{8,16},{16,24},{24,32},{32,40},{40,48},{48,56},{56,64},{64,7... | collective-permute-start | bytes 393224 | tf_op jit(solution)/shard_map/ppermute | solution.py:16
  697.8 7.6 %collective-permute-start.7 = (bf16[10,1,512]{2,1,0:T(2,128)(2,1)S(1)}, bf16[10,1,512]{2,1,0:T(2,128)(2,1)S(1)}, u32[]{:S(2)}, u32[]{:S(2)}) collective-permute-start(bf16[10,1,512]{2,1,0:T(2,128)(2,1)S(1)} %get-tuple-element.12), channel_id=1, source_target_pairs={{1,0},{2,1},{3,2},{4,3},{5,4},{6,5},{7,6},{9,8},{10,9},{11,10},{12... | collective-permute-start | bytes 30728 | tf_op jit(solution)/shard_map/ppermute | solution.py:19
  700.5 4.8 collective-permute-start.6
  708.3 1.7 copy-start.2
Sparse Core Ops, SparseCore 0:
  39.4 258.1 all-reduce.2
  300.2 378.9 all-gather.2
where the time goes:
time: 726 us; the launch traced here: 720 us
  waiting for transfers between devices  645 us (89%)
  starting transfers between devices  26.5 us (4%)
  local copies, waits for them, and re-layouts  15 us (2%)
  between operations  14.4 us (2%)
  matrix products  13.3 us (2%)
    all_gather x1, waiting for transfers between devices, on_device(): error_full = lax.all_gather(error_own, ('rows', 'cols'), axis=0, tiled=True)  380 us
    unnamed x3, waiting for transfers between devices  258 us
    ppermute x4, starting transfers between devices, padded_2(): lax.ppermute(lax.slice_in_dim(block, block.shape[dim] - width, None, axis...  19.2 us
  transfers between devices with their start and end apart: 10, of which 4 were waited for; matrix products, arithmetic and copies ran while one was open for 1% of the time, Pallas kernels for 0%

commit v1 on v0

v1 whole, which is shorter than its diff:
```python
import math

import jax
import jax.numpy as jnp
from jax import lax
from jax.experimental import pallas as pl
from jax.experimental.pallas import tpu as pltpu
from jax.sharding import PartitionSpec as P

MESH = pl.DeviceIdType.MESH
f32, bf16 = jnp.float32, jnp.bfloat16
C0 = math.sqrt(2.0 / math.pi)
C1 = C0 * 0.044715
TR, TC, CI, CO = 8, 128, 256, 512
NPIX = 262144
NR, NC = 32, 8
RING = 10 * TC


def gelu_pair(v):
    square = v * v
    half = 0.5 + 0.5 * jnp.tanh(v * (C0 + C1 * square))
    feat = v * half
    slope = half + feat * (1.0 - half) * (2.0 * C0 + 6.0 * C1 * square)
    return feat, slope


def kernel(
    canvas, weight, bias, target, gram_out, grad_out,
    xs, left, right, wv, feats, deriv, gp, gring, ringx, pan, s0, r0, s1, r1, s2, r2, gf,
    sym, tt, gfull, t2, tz, tc, tb, outv, outg, edge,
    lsem, hsend, hrecv, send, xrecv, zrecv, arecv, frecv, srecv, tsrecv, tzrecv, txrecv, tfrecv, osem,
):
    r = lax.axis_index("rows")
    c = lax.axis_index("cols")
    xy, zl, core, zh = r % 16, r // 16, c % 2, c // 2
    z = zh * 2 + zl
    sib = (r, c + 1 - 2 * core)

    def xyp(j):
        return (zl * 16 + (xy + j) % 16, c)

    def zp(j):
        z2 = (z + j) % 8
        return ((z2 % 2) * 16 + xy, (z2 // 2) * 2 + core)

    def rcopy(src, dst, ssem, rsem, dev):
        return pltpu.make_async_remote_copy(
            src_ref=src, dst_ref=dst, send_sem=ssem, recv_sem=rsem, device_id=dev, device_id_type=MESH
        )

    ld_canvas = pltpu.make_async_copy(canvas, xs.at[1, pl.ds(2, TR)], lsem.at[0])
    ld_weight = pltpu.make_async_copy(weight, wv, lsem.at[1])
    ld_target = pltpu.make_async_copy(target, t2.at[core], lsem.at[2])
    ld_canvas.start()
    ld_weight.start()
    ld_target.start()

    has_up, has_dn, has_lf, has_rt = r > 0, r < NR - 1, c > 0, c < NC - 1
    halo = []
    for dr in (-1, 0, 1):
        for dc in (-1, 0, 1):
            if dr == 0 and dc == 0:
                continue
            cond = None
            for step, flag in ((dr, (has_up, has_dn)), (dc, (has_lf, has_rt))):
                if step:
                    this = flag[0] if step < 0 else flag[1]
                    cond = this if cond is None else jnp.logical_and(cond, this)
            halo.append((dr, dc, cond))
    bar = pltpu.get_barrier_semaphore()
    count = jnp.int32(23)
    for dr, dc, cond in halo:
        count = count + jnp.where(cond, 1, 0)

        @pl.when(cond)
        def _():
            pl.semaphore_signal(bar, inc=1, device_id=(r + dr, c + dc), device_id_type=MESH)

    pl.semaphore_signal(bar, inc=1, device_id=sib, device_id_type=MESH)
    for j in range(1, 16):
        pl.semaphore_signal(bar, inc=1, device_id=xyp(j), device_id_type=MESH)
    for j in range(1, 8):
        pl.semaphore_signal(bar, inc=1, device_id=zp(j), device_id_type=MESH)
    pl.semaphore_wait(bar, count)

    def halo_copy(k, dr, dc):
        rows_src = pl.ds(0, 2) if dr < 0 else (pl.ds(TR - 2, 2) if dr > 0 else pl.ds(0, TR))
        rows_dst = pl.ds(TR + 2, 2) if dr < 0 else (pl.ds(0, 2) if dr > 0 else pl.ds(2, TR))
        if dc == 0:
            src, dst = canvas.at[rows_src], xs.at[1, rows_dst]
        elif dc < 0:
            src, dst = canvas.at[rows_src, pl.ds(0, 8)], right.at[rows_dst]
        else:
            src, dst = canvas.at[rows_src, pl.ds(TC - 8, 8)], left.at[rows_dst]
        return rcopy(src, dst, hsend.at[k], hrecv.at[k], (r + dr, c + dc))

    for k, (dr, dc, cond) in enumerate(halo):

        @pl.when(cond)
        def _():
            halo_copy(k, dr, dc).start()

    t_sib = rcopy(target, t2.at[core], send.at[0], tsrecv, sib)
    t_sib.start()

    @pl.when(r == 0)
    def _():
        xs[1, 0:2] = jnp.zeros((2, TC, CI), bf16)
        left[0:2] = jnp.zeros((2, 8, CI), bf16)
        right[0:2] = jnp.zeros((2, 8, CI), bf16)

    @pl.when(r == NR - 1)
    def _():
        xs[1, TR + 2 : TR + 4] = jnp.zeros((2, TC, CI), bf16)
        left[TR + 2 : TR + 4] = jnp.zeros((2, 8, CI), bf16)
        right[TR + 2 : TR + 4] = jnp.zeros((2, 8, CI), bf16)

    @pl.when(c == 0)
    def _():
        left[...] = jnp.zeros((TR + 4, 8, CI), bf16)

    @pl.when(c == NC - 1)
    def _():
        right[...] = jnp.zeros((TR + 4, 8, CI), bf16)

    ld_canvas.wait()
    ld_target.wait()
    for k, (dr, dc, cond) in enumerate(halo):

        @pl.when(cond)
        def _():
            halo_copy(7 - k, -dr, -dc).wait_recv()

    t_sib.wait_recv()
    quads = []
    for b in range(2):
        for q in range(2):
            rows2 = t2[q]
            quads.append(
                jnp.where(core == 0, rows2[:, b * 128 : b * 128 + 128], rows2[:, 256 + b * 128 : 384 + b * 128])
            )
    tz[z] = jnp.concatenate(quads, axis=0)
    t_z = [rcopy(tz.at[z], tz.at[z], send.at[j], tzrecv.at[j], zp(j)) for j in range(1, 8)]
    for cp in t_z:
        cp.start()

    lane_row = lax.broadcasted_iota(jnp.int32, (TC, CI), 0)

    def shift_row(i, carry):
        row = xs[1, i].astype(f32)
        lcol = left[i].astype(f32)[7:8]
        rcol = right[i].astype(f32)[0:1]
        xs[0, i] = jnp.where(lane_row == 0, lcol, pltpu.roll(row, 1, axis=0)).astype(bf16)
        xs[2, i] = jnp.where(lane_row == TC - 1, rcol, pltpu.roll(row, TC - 1, axis=0)).astype(bf16)
        return carry

    lax.fori_loop(0, TR + 4, shift_row, 0)
    ld_weight.wait()
    bias_row = bias[...].astype(f32).reshape(1, CO)
    wflat = wv.reshape(9 * CI, CO)

    def conv(parts):
        lhs = jnp.concatenate(parts, axis=1)
        return jnp.dot(lhs, wflat[...], preferred_element_type=f32) + bias_row

    def emit(start, v, scale):
        feat, slope = gelu_pair(v)
        feats[pl.ds(start, v.shape[0])] = feat.astype(bf16)
        deriv[pl.ds(start, v.shape[0])] = slope * scale
        return feat.astype(bf16)

    scale = 1.0 / math.sqrt(CO)
    pan[...] = jnp.zeros(pan.shape, f32)

    def main_tile(t, carry):
        h = 2 * t
        parts = [xs[b, pl.ds(h + a + 1, 2)].reshape(2 * TC, CI) for a in range(3) for b in range(3)]
        feat = emit(pl.multiple_of((h + 1) * TC, TC), conv(parts), scale)
        lo, hi = feat[:, 0:256], feat[:, 256:512]
        for q, (one, two) in enumerate(((lo, lo), (lo, hi), (hi, hi))):
            prod = lax.dot_general(one, two, (((0,), (0,)), ((), ())), preferred_element_type=f32)
            for s in range(2):
                at = (2 * q + s) * 256
                pan[at : at + 256] = pan[at : at + 256] + prod[:, s * 128 : s * 128 + 128]
        return carry

    lax.fori_loop(0, TR // 2, main_tile, 0)

    own_half = pl.multiple_of(core * 768, 768)
    other_half = pl.multiple_of((1 - core) * 768, 768)
    s0[...] = pan[pl.ds(other_half, 768)].astype(bf16)
    g_sib = rcopy(s0, r0, send.at[8], srecv, sib)
    g_sib.start()
    for cp in t_z:
        cp.wait_recv()
    for zz in range(2):
        for b in range(2):
            rows16 = jnp.concatenate([tz[q * 2 + zz][b * 4 : b * 4 + 4] for q in range(4)], axis=0)
            tc[(zz * 2 + b) * 16 : (zz * 2 + b) * 16 + 16] = rows16.astype(bf16)
    g_sib.wait_recv()
    half = pan[pl.ds(own_half, 768)] + r0[...].astype(f32)
    s1[...] = half.astype(bf16)
    pan[pl.ds(own_half, 768)] = half

    g_xy = []
    for j in range(1, 16):
        k = (xy + j) % 16
        g_xy.append(
            rcopy(s1.at[pl.ds(pl.multiple_of(48 * k, 16), 48)], r1.at[j], send.at[8 + j], xrecv.at[j], xyp(j))
        )
    for cp in g_xy:
        cp.start()
    own_t = tb.at[core, pl.ds(pl.multiple_of(64 * xy, 64), 64)]
    t_xy = [rcopy(tc, own_t, send.at[23 + j], txrecv.at[j], xyp(j)) for j in range(1, 16)]
    for cp in t_xy:
        cp.start()
    tb[core, pl.ds(pl.multiple_of(64 * xy, 64), 64)] = tc[...]

    up_on = jnp.where(has_up, scale, 0.0).astype(f32)
    dn_on = jnp.where(has_dn, scale, 0.0).astype(f32)
    lf_on = jnp.where(has_lf, 1.0, 0.0).astype(f32)
    rt_on = jnp.where(has_rt, 1.0, 0.0).astype(f32)
    emit(0, conv([xs[b, a] for a in range(3) for b in range(3)]), up_on)
    emit(9 * TC, conv([xs[b, 9 + a] for a in range(3) for b in range(3)]), dn_on)
    ringx[...] = jnp.zeros(ringx.shape, f32)
    lcols = left[...].astype(f32)
    rcols = right[...].astype(f32)
    first = xs[1, :, 0:8].astype(f32)
    last = xs[1, :, TC - 8 : TC].astype(f32)
    sides = ((lcols[:, 6], lcols[:, 7], first[:, 0]), (last[:, 7], rcols[:, 0], rcols[:, 1]))
    for s, cols in enumerate(sides):
        for b in range(3):
            for a in range(3):
                k = (a * 3 + b) * CI
                ringx[16 * s : 16 * s + 10, k : k + CI] = cols[b][a : a + 10]
    ring_row = lax.broadcasted_iota(jnp.int32, (32, CO), 0)
    side_on = jnp.where(ring_row < 16, lf_on, rt_on)
    pos = ring_row % 16
    row_on = jnp.where(pos == 0, up_on, jnp.where(pos == 9, dn_on, jnp.where(pos < 9, scale, 0.0)))
    emit(RING, conv([ringx[...].astype(bf16)]), side_on * row_on)

    own48 = pl.multiple_of(own_half + 48 * xy, 16)
    acc = pan[pl.ds(own48, 48)]
    for j in range(1, 16):
        g_xy[j - 1].wait_recv()
        acc = acc + r1[j].astype(f32)
    s2[...] = acc.astype(bf16)

    g_z = [rcopy(s2, r2.at[j], send.at[38 + j], zrecv.at[j], zp(j)) for j in range(1, 8)]
    for cp in g_z:
        cp.start()
    for cp in t_xy:
        cp.wait_recv()
    t_fw = rcopy(tb.at[core], tb.at[core], send.at[46], tfrecv, sib)
    t_fw.start()
    acc = s2[...].astype(f32)
    for j in range(1, 8):
        g_z[j - 1].wait_recv()
        acc = acc + r2[j].astype(f32)
    gf[pl.ds(own48, 48)] = (acc * (1.0 / NPIX)).astype(bf16)

    own_g = gf.at[pl.ds(own48, 48)]
    g_ag = [rcopy(own_g, own_g, send.at[46 + j], arecv.at[j], xyp(j)) for j in range(1, 16)]
    for cp in g_ag:
        cp.start()

    t_fw.wait_recv()

    def tquad(i, k):
        halves = []
        for q in range(2):
            blk = tb[k].reshape(16, 4, 16, 128)[:, i * 2 + q].reshape(256, 128)
            halves.append(blk.astype(f32))
        return jnp.concatenate(halves, axis=1)

    t01 = tquad(0, 1) + tquad(1, 0).T
    t00 = tquad(0, 0)
    t11 = tquad(1, 1)
    tt[0] = t00 + t00.T
    tt[1] = t01
    tt[2] = t01.T
    tt[3] = t11 + t11.T

    for cp in g_ag:
        cp.wait_recv()
    half_g = gf.at[pl.ds(own_half, 768)]
    g_fw = rcopy(half_g, half_g, send.at[62], frecv, sib)
    g_fw.start()
    g_fw.wait_recv()

    def gquad(q):
        return jnp.concatenate([gf[q * 512 : q * 512 + 256], gf[q * 512 + 256 : q * 512 + 512]], axis=1).astype(f32)

    g00, g01, g11 = gquad(0), gquad(1), gquad(2)
    g10 = g01.T
    sym[0:256, 0:256] = (2.0 * g00 - tt[0]).astype(bf16)
    sym[0:256, 256:512] = (2.0 * g01 - tt[1]).astype(bf16)
    sym[256:512, 0:256] = (2.0 * g10 - tt[2]).astype(bf16)
    sym[256:512, 256:512] = (2.0 * g11 - tt[3]).astype(bf16)
    gfull[0:256, 0:256] = g00
    gfull[0:256, 256:512] = g01
    gfull[256:512, 0:256] = g10
    gfull[256:512, 256:512] = g11

    def grad_tile(t, carry):
        at = pl.multiple_of(t * 256, 256)
        up = jnp.dot(feats[pl.ds(at, 256)], sym[...], preferred_element_type=f32)
        gp[pl.ds(at, 256)] = (up * deriv[pl.ds(at, 256)]).astype(bf16)
        return carry

    lax.fori_loop(0, 5, grad_tile, 0)
    upr = jnp.dot(feats[RING : RING + 32], sym[...], preferred_element_type=f32)
    gring[...] = (upr * deriv[RING : RING + 32]).astype(bf16).astype(f32)

    nt = (((1,), (1,)), ((), ()))
    for s, b in ((0, 2), (1, 0)):
        total = jnp.zeros((8, CI), f32)
        for a in range(3):
            rows8 = gring[16 * s + 2 - a : 16 * s + 10 - a].astype(bf16)
            total = total + lax.dot_general(rows8, wv[a * 3 + b], nt, preferred_element_type=f32)
        for h in range(TR):
            edge[s, h] = total[h : h + 1]

    def out_tile(t, carry):
        h = 2 * t
        total = jnp.zeros((2 * TC, 3 * CI), f32)
        for a in range(3):
            at = pl.multiple_of((h + 2 - a) * TC, TC)
            total = total + lax.dot_general(
                gp[pl.ds(at, 2 * TC)], wv[3 * a : 3 * a + 3].reshape(3 * CI, CO), nt, preferred_element_type=f32
            )
        for i in range(2):
            rows = total[i * TC : (i + 1) * TC]
            p0 = jnp.where(lane_row == TC - 1, edge[1, h + i], pltpu.roll(rows[:, 0:CI], TC - 1, axis=0))
            p2 = jnp.where(lane_row == 0, edge[0, h + i], pltpu.roll(rows[:, 2 * CI :], 1, axis=0))
            outv[h + i] = (rows[:, CI : 2 * CI] + p0 + p2).astype(bf16)
        pltpu.make_async_copy(outv.at[pl.ds(h, 2)], grad_out.at[pl.ds(h, 2)], osem.at[t]).start()
        return carry

    lax.fori_loop(0, TR // 2, out_tile, 0)

    own_row = zl * 256 + xy * 16 + zh * 4 + core * 2
    rows8 = gfull[pl.ds(pl.multiple_of((own_row // 8) * 8, 8), 8)]
    sub = lax.broadcasted_iota(jnp.int32, (8, CO), 0)
    for k in range(2):
        outg[k : k + 1] = jnp.sum(jnp.where(sub == own_row % 8 + k, rows8, 0.0), axis=0, keepdims=True)
    g_out = pltpu.make_async_copy(outg, gram_out, osem.at[4])
    g_out.start()
    g_out.wait()
    for t in range(TR // 2):
        pltpu.make_async_copy(outv.at[pl.ds(2 * t, 2)], grad_out.at[pl.ds(2 * t, 2)], osem.at[t]).wait()
    for k, (dr, dc, cond) in enumerate(halo):

        @pl.when(cond)
        def _():
            halo_copy(k, dr, dc).wait_send()

    for cp in [t_sib, g_sib, t_fw, g_fw] + t_z + g_xy + t_xy + g_z + g_ag:
        cp.wait_send()


def on_device(canvas, conv_weight, conv_bias, target_gram):
    hbm = pl.BlockSpec(memory_space=pl.ANY)
    vmem = pl.BlockSpec(memory_space=pltpu.VMEM)
    dma = pltpu.SemaphoreType.DMA
    return pl.pallas_call(
        kernel,
        out_shape=(jax.ShapeDtypeStruct((2, CO), f32), jax.ShapeDtypeStruct((TR, TC, CI), bf16)),
        in_specs=[hbm, hbm, vmem, hbm],
        out_specs=(hbm, hbm),
        scratch_shapes=[
            pltpu.VMEM((3, TR + 4, TC, CI), bf16),
            pltpu.VMEM((TR + 4, 8, CI), bf16),
            pltpu.VMEM((TR + 4, 8, CI), bf16),
            pltpu.VMEM((9, CI, CO), bf16),
            pltpu.VMEM((RING + 32, CO), bf16),
            pltpu.VMEM((RING + 32, CO), f32),
            pltpu.VMEM((RING, CO), bf16),
            pltpu.VMEM((32, CO), f32),
            pltpu.VMEM((32, 9 * CI), f32),
            pltpu.VMEM((1536, 128), f32),
            pltpu.VMEM((768, 128), bf16),
            pltpu.VMEM((768, 128), bf16),
            pltpu.VMEM((768, 128), bf16),
            pltpu.VMEM((16, 48, 128), bf16),
            pltpu.VMEM((48, 128), bf16),
            pltpu.VMEM((8, 48, 128), bf16),
            pltpu.VMEM((1536, 128), bf16),
            pltpu.VMEM((CO, CO), bf16),
            pltpu.VMEM((4, 256, 256), f32),
            pltpu.VMEM((CO, CO), f32),
            pltpu.VMEM((2, 2, CO), f32),
            pltpu.VMEM((8, 8, 128), f32),
            pltpu.VMEM((64, 128), bf16),
            pltpu.VMEM((2, 1024, 128), bf16),
            pltpu.VMEM((TR, TC, CI), bf16),
            pltpu.VMEM((2, CO), f32),
            pltpu.VMEM((2, TR, 1, CI), f32),
            dma((3,)),
            dma((8,)),
            dma((8,)),
            dma((63,)),
            dma((16,)),
            dma((8,)),
            dma((16,)),
            dma,
            dma,
            dma,
            dma((8,)),
            dma((16,)),
            dma,
            dma((5,)),
        ],
        compiler_params=pltpu.CompilerParams(
            collective_id=0, has_side_effects=True, vmem_limit_bytes=56 * 1024 * 1024
        ),
        name="style_grad",
    )(canvas, conv_weight.reshape(9, CI, CO), conv_bias, target_gram)


def solution(mesh):
    return jax.shard_map(
        on_device,
        mesh=mesh,
        in_specs=(P("rows", "cols", None), P(), P(), P(("rows", "cols"), None)),
        out_specs=(P(("rows", "cols"), None), P("rows", "cols", None)),
        check_vma=False,
    )
```

time: 726 us -> 55.3 us (0.08)
  waiting for transfers between devices: 645 us -> 0 us
  Pallas kernels: 0 us -> 51.3 us
  starting transfers between devices: 26.5 us -> 0 us
  between operations: 14.4 us -> 0.64 us
  matrix products: 13.3 us -> 0 us
  local copies, waits for them, and re-layouts: 15 us -> 3.13 us
    all_gather x1 -> x0, waiting for transfers between devices: 380 us -> none  [on_device(): error_full = lax.all_gather(error_own, ('rows', 'cols'), axis=0, tiled=True)]
    unnamed x3 -> x0, waiting for transfers between devices: 258 us -> none
    pallas_call x0 -> x1, Pallas kernels: none -> 51.3 us  [on_device(): pl.pallas_call(kernel, out_shape=(jax.ShapeDtypeStruct((2, CO), f32), jax...]
    ppermute x8 -> x0, starting transfers between devices: 26.4 us -> none  [the longest x4 19.2 us: padded_2(): lax.ppermute(lax.slice_in_dim(block, block.shape[dim] - width, None, axis...]
    dot_general x4 -> x0, matrix products: 13.3 us -> none  [the longest x1 4.52 us: on_device(): jnp.dot(features, symmetric, preferred_element_type=jnp.float32)]
    unnamed x24 -> x2, local copies, waits for them, and re-layouts: 10.8 us -> 3.13 us
  transfers between devices with their start and end apart: 10 -> 0, of which waited for: 4 -> 0; matrix products, arithmetic and copies ran while one was open for 1% -> 0% of each run, Pallas kernels for 0% -> 0%
where the time goes in v1:
time: 55.3 us; the launch traced here: 55.1 us
  Pallas kernels  51.3 us (93%)
  local copies, waits for them, and re-layouts  3.13 us (6%)
  between operations  0.64 us (1%)
    pallas_call x1, Pallas kernels, on_device(): pl.pallas_call(kernel, out_shape=(jax.ShapeDtypeStruct((2, CO), f32), jax...  51.3 us
    unnamed x2, local copies, waits for them, and re-layouts  3.13 us

profile of v1, /device:TPU:1, one launch (start us, length us, event | category | flops | bytes accessed | tf_op | source)
XLA Modules:
  0.0 55.1 jit_solution(18275671168534319429)
XLA Ops:
  0.6 51.3 %style_grad.1 = (f32[2,512]{1,0:T(2,128)}, bf16[8,128,256]{2,1,0:T(8,128)(2,1)}) custom-call(bf16[8,128,256]{2,1,0:T(8,128)(2,1)} %canvas.1, bf16[9,256,512]{2,1,0:T(8,128)(2,1)} %bitcast.1, bf16[512]{0:T(512)(128)(2,1)} %bias.1, f32[2,512]{1,0:T(2,128)} %target.1), custom_call_target="tpu_custom_call" | custom-call | tf_op jit(solution)/shard_map/style_grad/pallas_call | solution.py:367
  52.0 1.3 %copy.8 = f32[2,512]{1,0:T(2,128)} copy(f32[2,512]{1,0:T(2,128)} %get-tuple-element.4) | data formatting | bytes 8192
  53.2 1.9 %copy.9 = bf16[8,128,256]{2,1,0:T(8,128)(2,1)} copy(bf16[8,128,256]{2,1,0:T(8,128)(2,1)} %get-tuple-element.5) | data formatting | bytes 1048576

commit v2 on v1

--- a/solution.py
+++ b/solution.py
@@ -15,6 +15,10 @@
 NPIX = 262144
 NR, NC = 32, 8
 RING = 10 * TC
+XY_STEPS = sorted(
+    ((i, j) for i in range(4) for j in range(4) if i or j), key=lambda s: (-min(s[0], 4 - s[0]) - min(s[1], 4 - s[1]), s)
+)
+Z_STEPS = (4, 3, 5, 2, 6, 1, 7)
 
 
 def gelu_pair(v):
@@ -27,7 +31,7 @@
 
 def kernel(
     canvas, weight, bias, target, gram_out, grad_out,
-    xs, left, right, wv, feats, deriv, gp, gring, ringx, pan, s0, r0, s1, r1, s2, r2, gf,
+    xs, left, right, wv, wt, feats, deriv, gp, gring, ringx, edgex, pan, s0, r0, s1, r1, s2, r2, gf,
     sym, tt, gfull, t2, tz, tc, tb, outv, outg, edge,
     lsem, hsend, hrecv, send, xrecv, zrecv, arecv, frecv, srecv, tsrecv, tzrecv, txrecv, tfrecv, osem,
 ):
@@ -37,11 +41,17 @@
     z = zh * 2 + zl
     sib = (r, c + 1 - 2 * core)
 
+    x, y = xy % 4, xy // 4
+
+    def xyk(j, sign=1):
+        dx, dy = XY_STEPS[j - 1]
+        return (x + sign * dx + 4) % 4 + 4 * ((y + sign * dy + 4) % 4)
+
     def xyp(j):
-        return (zl * 16 + (xy + j) % 16, c)
+        return (zl * 16 + xyk(j), c)
 
     def zp(j):
-        z2 = (z + j) % 8
+        z2 = (z + Z_STEPS[j - 1]) % 8
         return ((z2 % 2) * 16 + xy, (z2 // 2) * 2 + core)
 
     def rcopy(src, dst, ssem, rsem, dev):
@@ -84,22 +94,32 @@
         pl.semaphore_signal(bar, inc=1, device_id=zp(j), device_id_type=MESH)
     pl.semaphore_wait(bar, count)
 
-    def halo_copy(k, dr, dc):
-        rows_src = pl.ds(0, 2) if dr < 0 else (pl.ds(TR - 2, 2) if dr > 0 else pl.ds(0, TR))
-        rows_dst = pl.ds(TR + 2, 2) if dr < 0 else (pl.ds(0, 2) if dr > 0 else pl.ds(2, TR))
+    kinds = [(dr, dc, 0) for dr, dc, _ in halo]
+    kinds = [(-1, 0, 0), (1, 0, 0)] + [k for k in kinds if k[1]] + [(-1, 0, 1), (1, 0, 1)]
+    flags = {(dr, dc): cond for dr, dc, cond in halo}
+
+    def halo_copy(dr, dc, outer):
+        k = kinds.index((dr, dc, outer))
         if dc == 0:
-            src, dst = canvas.at[rows_src], xs.at[1, rows_dst]
-        elif dc < 0:
-            src, dst = canvas.at[rows_src, pl.ds(0, 8)], right.at[rows_dst]
+            src = canvas.at[outer] if dr < 0 else canvas.at[TR - 1 - outer]
+            dst = xs.at[1, TR + 2 + outer] if dr < 0 else xs.at[1, 1 - outer]
         else:
-            src, dst = canvas.at[rows_src, pl.ds(TC - 8, 8)], left.at[rows_dst]
+            rows_src = pl.ds(0, 2) if dr < 0 else (pl.ds(TR - 2, 2) if dr > 0 else pl.ds(0, TR))
+            rows_dst = pl.ds(TR + 2, 2) if dr < 0 else (pl.ds(0, 2) if dr > 0 else pl.ds(2, TR))
+            if dc < 0:
+                src, dst = canvas.at[rows_src, pl.ds(0, 8)], right.at[rows_dst]
+            else:
+                src, dst = canvas.at[rows_src, pl.ds(TC - 8, 8)], left.at[rows_dst]
         return rcopy(src, dst, hsend.at[k], hrecv.at[k], (r + dr, c + dc))
 
-    for k, (dr, dc, cond) in enumerate(halo):
-
-        @pl.when(cond)
-        def _():
-            halo_copy(k, dr, dc).start()
+    def each_halo(some, act):
+        for dr, dc, outer in some:
+
+            @pl.when(flags[dr, dc])
+            def _():
+                act(dr, dc, outer)
+
+    each_halo(kinds, lambda dr, dc, outer: halo_copy(dr, dc, outer).start())
 
     t_sib = rcopy(target, t2.at[core], send.at[0], tsrecv, sib)
     t_sib.start()
@@ -124,14 +144,64 @@
     def _():
         right[...] = jnp.zeros((TR + 4, 8, CI), bf16)
 
+    lane_row = lax.broadcasted_iota(jnp.int32, (TC, CI), 0)
+
+    def shift_row(i):
+        row = xs[1, i].astype(f32)
+        xs[0, i] = pltpu.roll(row, 1, axis=0).astype(bf16)
+        xs[2, i] = pltpu.roll(row, TC - 1, axis=0).astype(bf16)
+
+    def shift_edges(i):
+        sub = lax.broadcasted_iota(jnp.int32, (16, CI), 0)
+        top = xs[0, i, 0:16].astype(f32)
+        xs[0, i, 0:16] = jnp.where(sub == 0, left[i].astype(f32)[7:8], top).astype(bf16)
+        bot = xs[2, i, TC - 16 : TC].astype(f32)
+        xs[2, i, TC - 16 : TC] = jnp.where(sub == 15, right[i].astype(f32)[0:1], bot).astype(bf16)
+
     ld_canvas.wait()
+
+    def shift_own(i, carry):
+        shift_row(i + 2)
+        return carry
+
+    lax.fori_loop(0, TR, shift_own, 0)
+    ld_weight.wait()
+    bias_row = bias[...].astype(f32).reshape(1, CO)
+    wflat = wv.reshape(9 * CI, CO)
+
+    def conv(parts):
+        lhs = jnp.concatenate(parts, axis=1)
+        return jnp.dot(lhs, wflat[...], preferred_element_type=f32) + bias_row
+
+    def taps(h, n):
+        return [xs[b, h + a + 1 : h + a + 1 + n].reshape(n * TC, CI) for a in range(3) for b in range(3)]
+
+    scale = 1.0 / math.sqrt(CO)
+
+    def add_gram(feat, fresh):
+        lo, hi = feat[:, 0:256], feat[:, 256:512]
+        for q, (one, two) in enumerate(((lo, lo), (lo, hi), (hi, hi))):
+            prod = lax.dot_general(one, two, (((0,), (0,)), ((), ())), preferred_element_type=f32)
+            for s in range(2):
+                at = (2 * q + s) * 256
+                part = prod[:, s * 128 : s * 128 + 128]
+                pan[at : at + 256] = part if fresh else pan[at : at + 256] + part
+
+    feat, slope = gelu_pair(conv(taps(1, 6)))
+    feats[2 * TC : 8 * TC] = feat.astype(bf16)
+    deriv[2 * TC : 8 * TC] = slope * scale
+    sub16 = lax.broadcasted_iota(jnp.int32, (16, CO), 0)
+
+    def put_row(ref, at, place, row):
+        old = ref[at : at + 16].astype(f32)
+        ref[at : at + 16] = jnp.where(sub16 == place, row, old).astype(ref.dtype)
+
+    for h in range(1, 7):
+        put_row(feats, (h + 1) * TC, 0, 0.0)
+        put_row(feats, (h + 2) * TC - 16, 15, 0.0)
+    add_gram(feats[2 * TC : 8 * TC], True)
+
     ld_target.wait()
-    for k, (dr, dc, cond) in enumerate(halo):
-
-        @pl.when(cond)
-        def _():
-            halo_copy(7 - k, -dr, -dc).wait_recv()
-
     t_sib.wait_recv()
     quads = []
     for b in range(2):
@@ -142,50 +212,38 @@
             )
     tz[z] = jnp.concatenate(quads, axis=0)
     t_z = [rcopy(tz.at[z], tz.at[z], send.at[j], tzrecv.at[j], zp(j)) for j in range(1, 8)]
+
+    each_halo(kinds[:8], lambda dr, dc, outer: halo_copy(-dr, -dc, outer).wait_recv())
     for cp in t_z:
         cp.start()
-
-    lane_row = lax.broadcasted_iota(jnp.int32, (TC, CI), 0)
-
-    def shift_row(i, carry):
-        row = xs[1, i].astype(f32)
-        lcol = left[i].astype(f32)[7:8]
-        rcol = right[i].astype(f32)[0:1]
-        xs[0, i] = jnp.where(lane_row == 0, lcol, pltpu.roll(row, 1, axis=0)).astype(bf16)
-        xs[2, i] = jnp.where(lane_row == TC - 1, rcol, pltpu.roll(row, TC - 1, axis=0)).astype(bf16)
-        return carry
-
-    lax.fori_loop(0, TR + 4, shift_row, 0)
-    ld_weight.wait()
-    bias_row = bias[...].astype(f32).reshape(1, CO)
-    wflat = wv.reshape(9 * CI, CO)
-
-    def conv(parts):
-        lhs = jnp.concatenate(parts, axis=1)
-        return jnp.dot(lhs, wflat[...], preferred_element_type=f32) + bias_row
-
-    def emit(start, v, scale):
-        feat, slope = gelu_pair(v)
-        feats[pl.ds(start, v.shape[0])] = feat.astype(bf16)
-        deriv[pl.ds(start, v.shape[0])] = slope * scale
-        return feat.astype(bf16)
-
-    scale = 1.0 / math.sqrt(CO)
-    pan[...] = jnp.zeros(pan.shape, f32)
-
-    def main_tile(t, carry):
-        h = 2 * t
-        parts = [xs[b, pl.ds(h + a + 1, 2)].reshape(2 * TC, CI) for a in range(3) for b in range(3)]
-        feat = emit(pl.multiple_of((h + 1) * TC, TC), conv(parts), scale)
-        lo, hi = feat[:, 0:256], feat[:, 256:512]
-        for q, (one, two) in enumerate(((lo, lo), (lo, hi), (hi, hi))):
-            prod = lax.dot_general(one, two, (((0,), (0,)), ((), ())), preferred_element_type=f32)
-            for s in range(2):
-                at = (2 * q + s) * 256
-                pan[at : at + 256] = pan[at : at + 256] + prod[:, s * 128 : s * 128 + 128]
-        return carry
-
-    lax.fori_loop(0, TR // 2, main_tile, 0)
+    shift_row(1)
+    shift_row(TR + 2)
+    for i in range(1, TR + 3):
+        shift_edges(i)
+    first = xs[1, 1 : TR + 3, 0:8].astype(f32)
+    last = xs[1, 1 : TR + 3, TC - 8 : TC].astype(f32)
+    lcols = left[...].astype(f32)
+    rcols = right[...].astype(f32)
+    mid_l, mid_r = lcols[1 : TR + 3], rcols[1 : TR + 3]
+    sides = ((mid_l[:, 7], first[:, 0], first[:, 1]), (last[:, 6], last[:, 7], mid_r[:, 0]))
+    for s, cols in enumerate(sides):
+        for b in range(3):
+            for a in range(3):
+                k = (a * 3 + b) * CI
+                edgex[8 * s : 8 * s + 8, k : k + CI] = cols[b][a : a + 8]
+    lhs = [
+        jnp.concatenate([one, two, edgex[:, k * CI : k * CI + CI].astype(bf16)], axis=0)
+        for k, (one, two) in enumerate(zip(taps(0, 1), taps(7, 1), strict=True))
+    ]
+    feat, slope = gelu_pair(conv(lhs))
+    slope = slope * scale
+    feats[TC : 2 * TC] = feat[0:TC].astype(bf16)
+    deriv[TC : 2 * TC] = slope[0:TC]
+    feats[8 * TC : 9 * TC] = feat[TC : 2 * TC].astype(bf16)
+    deriv[8 * TC : 9 * TC] = slope[TC : 2 * TC]
+    edge_f, edge_d = feat[2 * TC :], slope[2 * TC :]
+    corner = jnp.logical_or(sub16 % 8 == 0, sub16 % 8 == 7)
+    add_gram(jnp.concatenate([feat[0 : 2 * TC], jnp.where(corner, 0.0, edge_f)], axis=0).astype(bf16), False)
 
     own_half = pl.multiple_of(core * 768, 768)
     other_half = pl.multiple_of((1 - core) * 768, 768)
@@ -205,7 +263,7 @@
 
     g_xy = []
     for j in range(1, 16):
-        k = (xy + j) % 16
+        k = xyk(j)
         g_xy.append(
             rcopy(s1.at[pl.ds(pl.multiple_of(48 * k, 16), 48)], r1.at[j], send.at[8 + j], xrecv.at[j], xyp(j))
         )
@@ -217,15 +275,19 @@
         cp.start()
     tb[core, pl.ds(pl.multiple_of(64 * xy, 64), 64)] = tc[...]
 
+    for h in range(1, 7):
+        for s, (at, place) in enumerate((((h + 1) * TC, 0), ((h + 2) * TC - 16, 15))):
+            put_row(feats, at, place, edge_f[8 * s + h : 8 * s + h + 1])
+            put_row(deriv, at, place, edge_d[8 * s + h : 8 * s + h + 1])
+    each_halo(kinds[8:], lambda dr, dc, outer: halo_copy(-dr, -dc, outer).wait_recv())
+    for i in (0, TR + 3):
+        shift_row(i)
+        shift_edges(i)
     up_on = jnp.where(has_up, scale, 0.0).astype(f32)
     dn_on = jnp.where(has_dn, scale, 0.0).astype(f32)
     lf_on = jnp.where(has_lf, 1.0, 0.0).astype(f32)
     rt_on = jnp.where(has_rt, 1.0, 0.0).astype(f32)
-    emit(0, conv([xs[b, a] for a in range(3) for b in range(3)]), up_on)
-    emit(9 * TC, conv([xs[b, 9 + a] for a in range(3) for b in range(3)]), dn_on)
     ringx[...] = jnp.zeros(ringx.shape, f32)
-    lcols = left[...].astype(f32)
-    rcols = right[...].astype(f32)
     first = xs[1, :, 0:8].astype(f32)
     last = xs[1, :, TC - 8 : TC].astype(f32)
     sides = ((lcols[:, 6], lcols[:, 7], first[:, 0]), (last[:, 7], rcols[:, 0], rcols[:, 1]))
@@ -234,11 +296,21 @@
             for a in range(3):
                 k = (a * 3 + b) * CI
                 ringx[16 * s : 16 * s + 10, k : k + CI] = cols[b][a : a + 10]
+    lhs = [
+        jnp.concatenate([one, two, ringx[:, k * CI : k * CI + CI].astype(bf16)], axis=0)
+        for k, (one, two) in enumerate(zip(taps(-1, 1), taps(8, 1), strict=True))
+    ]
+    feat, slope = gelu_pair(conv(lhs))
+    feats[0:TC] = feat[0:TC].astype(bf16)
+    deriv[0:TC] = slope[0:TC] * up_on
+    feats[9 * TC : 10 * TC] = feat[TC : 2 * TC].astype(bf16)
+    deriv[9 * TC : 10 * TC] = slope[TC : 2 * TC] * dn_on
     ring_row = lax.broadcasted_iota(jnp.int32, (32, CO), 0)
     side_on = jnp.where(ring_row < 16, lf_on, rt_on)
     pos = ring_row % 16
     row_on = jnp.where(pos == 0, up_on, jnp.where(pos == 9, dn_on, jnp.where(pos < 9, scale, 0.0)))
-    emit(RING, conv([ringx[...].astype(bf16)]), side_on * row_on)
+    feats[RING : RING + 32] = feat[2 * TC :].astype(bf16)
+    deriv[RING : RING + 32] = slope[2 * TC :] * (side_on * row_on)
 
     own48 = pl.multiple_of(own_half + 48 * xy, 16)
     acc = pan[pl.ds(own48, 48)]
@@ -254,6 +326,9 @@
         cp.wait_recv()
     t_fw = rcopy(tb.at[core], tb.at[core], send.at[46], tfrecv, sib)
     t_fw.start()
+    for a in range(3):
+        for b in range(3):
+            wt[a * CO : a * CO + CO, b * CI : b * CI + CI] = wv[3 * a + b].T
     acc = s2[...].astype(f32)
     for j in range(1, 8):
         g_z[j - 1].wait_recv()
@@ -282,12 +357,15 @@
     tt[2] = t01.T
     tt[3] = t11 + t11.T
 
-    for cp in g_ag:
+    g_fw = [rcopy(own_g, own_g, send.at[62], frecv.at[0], sib)]
+    g_fw[0].start()
+    for j in range(15, 0, -1):
+        g_ag[j - 1].wait_recv()
+        got = gf.at[pl.ds(pl.multiple_of(own_half + 48 * xyk(j, -1), 16), 48)]
+        g_fw.append(rcopy(got, got, send.at[62 + j], frecv.at[j], sib))
+        g_fw[-1].start()
+    for cp in g_fw:
         cp.wait_recv()
-    half_g = gf.at[pl.ds(own_half, 768)]
-    g_fw = rcopy(half_g, half_g, send.at[62], frecv, sib)
-    g_fw.start()
-    g_fw.wait_recv()
 
     def gquad(q):
         return jnp.concatenate([gf[q * 512 : q * 512 + 256], gf[q * 512 + 256 : q * 512 + 512]], axis=1).astype(f32)
@@ -303,42 +381,35 @@
     gfull[256:512, 0:256] = g10
     gfull[256:512, 256:512] = g11
 
-    def grad_tile(t, carry):
-        at = pl.multiple_of(t * 256, 256)
-        up = jnp.dot(feats[pl.ds(at, 256)], sym[...], preferred_element_type=f32)
-        gp[pl.ds(at, 256)] = (up * deriv[pl.ds(at, 256)]).astype(bf16)
-        return carry
-
-    lax.fori_loop(0, 5, grad_tile, 0)
+    for t in range(2):
+        at = t * 5 * TC
+        up = jnp.dot(feats[at : at + 5 * TC], sym[...], preferred_element_type=f32)
+        gp[at : at + 5 * TC] = (up * deriv[at : at + 5 * TC]).astype(bf16)
     upr = jnp.dot(feats[RING : RING + 32], sym[...], preferred_element_type=f32)
     gring[...] = (upr * deriv[RING : RING + 32]).astype(bf16).astype(f32)
 
-    nt = (((1,), (1,)), ((), ()))
     for s, b in ((0, 2), (1, 0)):
         total = jnp.zeros((8, CI), f32)
         for a in range(3):
             rows8 = gring[16 * s + 2 - a : 16 * s + 10 - a].astype(bf16)
-            total = total + lax.dot_general(rows8, wv[a * 3 + b], nt, preferred_element_type=f32)
+            total = total + jnp.dot(
+                rows8, wt[a * CO : a * CO + CO, b * CI : b * CI + CI], preferred_element_type=f32
+            )
         for h in range(TR):
             edge[s, h] = total[h : h + 1]
 
-    def out_tile(t, carry):
-        h = 2 * t
-        total = jnp.zeros((2 * TC, 3 * CI), f32)
-        for a in range(3):
-            at = pl.multiple_of((h + 2 - a) * TC, TC)
-            total = total + lax.dot_general(
-                gp[pl.ds(at, 2 * TC)], wv[3 * a : 3 * a + 3].reshape(3 * CI, CO), nt, preferred_element_type=f32
-            )
-        for i in range(2):
+    outs = []
+    for t in range(2):
+        lhs = jnp.concatenate([gp[(4 * t + 2 - a) * TC : (4 * t + 6 - a) * TC] for a in range(3)], axis=1)
+        total = jnp.dot(lhs, wt[...], preferred_element_type=f32)
+        for i in range(4):
+            h = 4 * t + i
             rows = total[i * TC : (i + 1) * TC]
-            p0 = jnp.where(lane_row == TC - 1, edge[1, h + i], pltpu.roll(rows[:, 0:CI], TC - 1, axis=0))
-            p2 = jnp.where(lane_row == 0, edge[0, h + i], pltpu.roll(rows[:, 2 * CI :], 1, axis=0))
-            outv[h + i] = (rows[:, CI : 2 * CI] + p0 + p2).astype(bf16)
-        pltpu.make_async_copy(outv.at[pl.ds(h, 2)], grad_out.at[pl.ds(h, 2)], osem.at[t]).start()
-        return carry
-
-    lax.fori_loop(0, TR // 2, out_tile, 0)
+            p0 = jnp.where(lane_row == TC - 1, edge[1, h], pltpu.roll(rows[:, 0:CI], TC - 1, axis=0))
+            p2 = jnp.where(lane_row == 0, edge[0, h], pltpu.roll(rows[:, 2 * CI :], 1, axis=0))
+            outv[h] = (rows[:, CI : 2 * CI] + p0 + p2).astype(bf16)
+        outs.append(pltpu.make_async_copy(outv.at[pl.ds(4 * t, 4)], grad_out.at[pl.ds(4 * t, 4)], osem.at[t]))
+        outs[t].start()
 
     own_row = zl * 256 + xy * 16 + zh * 4 + core * 2
     rows8 = gfull[pl.ds(pl.multiple_of((own_row // 8) * 8, 8), 8)]
@@ -348,25 +419,30 @@
     g_out = pltpu.make_async_copy(outg, gram_out, osem.at[4])
     g_out.start()
     g_out.wait()
-    for t in range(TR // 2):
-        pltpu.make_async_copy(outv.at[pl.ds(2 * t, 2)], grad_out.at[pl.ds(2 * t, 2)], osem.at[t]).wait()
-    for k, (dr, dc, cond) in enumerate(halo):
-
-        @pl.when(cond)
-        def _():
-            halo_copy(k, dr, dc).wait_send()
-
-    for cp in [t_sib, g_sib, t_fw, g_fw] + t_z + g_xy + t_xy + g_z + g_ag:
+    for cp in outs:
+        cp.wait()
+    each_halo(kinds, lambda dr, dc, outer: halo_copy(dr, dc, outer).wait_send())
+    for cp in [t_sib, g_sib, t_fw] + g_fw + t_z + g_xy + t_xy + g_z + g_ag:
         cp.wait_send()
+
+
+def finish(gram, grad, gram_out, grad_out, sem):
+    one = pltpu.make_async_copy(gram, gram_out, sem.at[0])
+    two = pltpu.make_async_copy(grad, grad_out, sem.at[1])
+    one.start()
+    two.start()
+    one.wait()
+    two.wait()
 
 
 def on_device(canvas, conv_weight, conv_bias, target_gram):
     hbm = pl.BlockSpec(memory_space=pl.ANY)
     vmem = pl.BlockSpec(memory_space=pltpu.VMEM)
     dma = pltpu.SemaphoreType.DMA
-    return pl.pallas_call(
+    shapes = (jax.ShapeDtypeStruct((2, CO), f32), jax.ShapeDtypeStruct((TR, TC, CI), bf16))
+    gram, grad = pl.pallas_call(
         kernel,
-        out_shape=(jax.ShapeDtypeStruct((2, CO), f32), jax.ShapeDtypeStruct((TR, TC, CI), bf16)),
+        out_shape=shapes,
         in_specs=[hbm, hbm, vmem, hbm],
         out_specs=(hbm, hbm),
         scratch_shapes=[
@@ -374,11 +450,13 @@
             pltpu.VMEM((TR + 4, 8, CI), bf16),
             pltpu.VMEM((TR + 4, 8, CI), bf16),
             pltpu.VMEM((9, CI, CO), bf16),
+            pltpu.VMEM((3 * CO, 3 * CI), bf16),
             pltpu.VMEM((RING + 32, CO), bf16),
             pltpu.VMEM((RING + 32, CO), f32),
             pltpu.VMEM((RING, CO), bf16),
             pltpu.VMEM((32, CO), f32),
             pltpu.VMEM((32, 9 * CI), f32),
+            pltpu.VMEM((16, 9 * CI), f32),
             pltpu.VMEM((1536, 128), f32),
             pltpu.VMEM((768, 128), bf16),
             pltpu.VMEM((768, 128), bf16),
@@ -398,13 +476,13 @@
             pltpu.VMEM((2, CO), f32),
             pltpu.VMEM((2, TR, 1, CI), f32),
             dma((3,)),
-            dma((8,)),
-            dma((8,)),
-            dma((63,)),
+            dma((10,)),
+            dma((10,)),
+            dma((78,)),
             dma((16,)),
             dma((8,)),
             dma((16,)),
-            dma,
+            dma((16,)),
             dma,
             dma,
             dma((8,)),
@@ -417,6 +495,9 @@
         ),
         name="style_grad",
     )(canvas, conv_weight.reshape(9, CI, CO), conv_bias, target_gram)
+    return pl.pallas_call(
+        finish, out_shape=shapes, in_specs=[hbm, hbm], out_specs=(hbm, hbm), scratch_shapes=[dma((2,))], name="finish"
+    )(gram, grad)
 
 
 def solution(mesh):

time: 55.3 us -> 63.4 us (1.15)
  Pallas kernels: 51.3 us -> 62.6 us
  local copies, waits for them, and re-layouts: 3.13 us -> 0 us
    pallas_call x1 -> x2, Pallas kernels: 51.3 us -> 62.6 us  [the longest x1 45.5 us: on_device(): pl.pallas_call(kernel, out_shape=shapes, in_specs=[hbm, hbm, vmem, hbm],...]
    unnamed x2 -> x0, local copies, waits for them, and re-layouts: 3.13 us -> none
where the time goes in v2:
time: 63.4 us; the launch traced here: 63.3 us
  Pallas kernels  62.6 us (99%)
  between operations  0.64 us (1%)
    pallas_call x1, Pallas kernels, on_device(): pl.pallas_call(kernel, out_shape=shapes, in_specs=[hbm, hbm, vmem, hbm],...  45.5 us
    pallas_call x1, Pallas kernels, on_device(): pl.pallas_call(finish, out_shape=shapes, in_specs=[hbm, hbm], out_specs=(...  17.1 us

profile of v2, /device:TPU:1, one launch (start us, length us, event | category | flops | bytes accessed | tf_op | source)
XLA Modules:
  0.0 63.3 jit_solution(12177550737866414896)
XLA Ops:
  0.6 45.5 %style_grad.1 = (f32[2,512]{1,0:T(2,128)}, bf16[8,128,256]{2,1,0:T(8,128)(2,1)}) custom-call(bf16[8,128,256]{2,1,0:T(8,128)(2,1)} %canvas.1, bf16[9,256,512]{2,1,0:T(8,128)(2,1)} %bitcast.1, bf16[512]{0:T(512)(128)(2,1)} %bias.1, f32[2,512]{1,0:T(2,128)} %target.1), custom_call_target="tpu_custom_call" | custom-call | tf_op jit(solution)/shard_map/style_grad/pallas_call | solution.py:443
  46.1 17.1 %finish.1 = (f32[2,512]{1,0:T(2,128)}, bf16[8,128,256]{2,1,0:T(8,128)(2,1)}) custom-call(f32[2,512]{1,0:T(2,128)} %get-tuple-element.4.gram, bf16[8,128,256]{2,1,0:T(8,128)(2,1)} %get-tuple-element.5.grad), custom_call_target="tpu_custom_call" | custom-call | tf_op jit(solution)/shard_map/finish/pallas_call | solution.py:498

commit v3 on v2

--- a/solution.py
+++ b/solution.py
@@ -30,10 +30,10 @@
 
 
 def kernel(
-    canvas, weight, bias, target, gram_out, grad_out,
+    canvas, weight, bias, target, outg, outv,
     xs, left, right, wv, wt, feats, deriv, gp, gring, ringx, edgex, pan, s0, r0, s1, r1, s2, r2, gf,
-    sym, tt, gfull, t2, tz, tc, tb, outv, outg, edge,
-    lsem, hsend, hrecv, send, xrecv, zrecv, arecv, frecv, srecv, tsrecv, tzrecv, txrecv, tfrecv, osem,
+    sym, tt, gfull, t2, tz, tc, tb, edge,
+    lsem, hsend, hrecv, send, xrecv, zrecv, arecv, frecv, srecv, tsrecv, tzrecv, txrecv, tfrecv,
 ):
     r = lax.axis_index("rows")
     c = lax.axis_index("cols")
@@ -165,42 +165,6 @@
         return carry
 
     lax.fori_loop(0, TR, shift_own, 0)
-    ld_weight.wait()
-    bias_row = bias[...].astype(f32).reshape(1, CO)
-    wflat = wv.reshape(9 * CI, CO)
-
-    def conv(parts):
-        lhs = jnp.concatenate(parts, axis=1)
-        return jnp.dot(lhs, wflat[...], preferred_element_type=f32) + bias_row
-
-    def taps(h, n):
-        return [xs[b, h + a + 1 : h + a + 1 + n].reshape(n * TC, CI) for a in range(3) for b in range(3)]
-
-    scale = 1.0 / math.sqrt(CO)
-
-    def add_gram(feat, fresh):
-        lo, hi = feat[:, 0:256], feat[:, 256:512]
-        for q, (one, two) in enumerate(((lo, lo), (lo, hi), (hi, hi))):
-            prod = lax.dot_general(one, two, (((0,), (0,)), ((), ())), preferred_element_type=f32)
-            for s in range(2):
-                at = (2 * q + s) * 256
-                part = prod[:, s * 128 : s * 128 + 128]
-                pan[at : at + 256] = part if fresh else pan[at : at + 256] + part
-
-    feat, slope = gelu_pair(conv(taps(1, 6)))
-    feats[2 * TC : 8 * TC] = feat.astype(bf16)
-    deriv[2 * TC : 8 * TC] = slope * scale
-    sub16 = lax.broadcasted_iota(jnp.int32, (16, CO), 0)
-
-    def put_row(ref, at, place, row):
-        old = ref[at : at + 16].astype(f32)
-        ref[at : at + 16] = jnp.where(sub16 == place, row, old).astype(ref.dtype)
-
-    for h in range(1, 7):
-        put_row(feats, (h + 1) * TC, 0, 0.0)
-        put_row(feats, (h + 2) * TC - 16, 15, 0.0)
-    add_gram(feats[2 * TC : 8 * TC], True)
-
     ld_target.wait()
     t_sib.wait_recv()
     quads = []
@@ -212,10 +176,46 @@
             )
     tz[z] = jnp.concatenate(quads, axis=0)
     t_z = [rcopy(tz.at[z], tz.at[z], send.at[j], tzrecv.at[j], zp(j)) for j in range(1, 8)]
-
-    each_halo(kinds[:8], lambda dr, dc, outer: halo_copy(-dr, -dc, outer).wait_recv())
     for cp in t_z:
         cp.start()
+
+    ld_weight.wait()
+    bias_row = bias[...].astype(f32).reshape(1, CO)
+    wflat = wv.reshape(9 * CI, CO)
+
+    def conv(parts):
+        lhs = jnp.concatenate(parts, axis=1)
+        return jnp.dot(lhs, wflat[...], preferred_element_type=f32) + bias_row
+
+    def taps(h, n):
+        return [xs[b, h + a + 1 : h + a + 1 + n].reshape(n * TC, CI) for a in range(3) for b in range(3)]
+
+    scale = 1.0 / math.sqrt(CO)
+
+    def add_gram(feat, fresh):
+        lo, hi = feat[:, 0:256], feat[:, 256:512]
+        for q, (one, two) in enumerate(((lo, lo), (lo, hi), (hi, hi))):
+            prod = lax.dot_general(one, two, (((0,), (0,)), ((), ())), preferred_element_type=f32)
+            for s in range(2):
+                at = (2 * q + s) * 256
+                part = prod[:, s * 128 : s * 128 + 128]
+                pan[at : at + 256] = part if fresh else pan[at : at + 256] + part
+
+    feat, slope = gelu_pair(conv(taps(1, 6)))
+    feats[2 * TC : 8 * TC] = feat.astype(bf16)
+    deriv[2 * TC : 8 * TC] = slope * scale
+    sub16 = lax.broadcasted_iota(jnp.int32, (16, CO), 0)
+
+    def put_row(ref, at, place, row):
+        old = ref[at : at + 16].astype(f32)
+        ref[at : at + 16] = jnp.where(sub16 == place, row, old).astype(ref.dtype)
+
+    for h in range(1, 7):
+        put_row(feats, (h + 1) * TC, 0, 0.0)
+        put_row(feats, (h + 2) * TC - 16, 15, 0.0)
+    add_gram(feats[2 * TC : 8 * TC], True)
+
+    each_halo(kinds[:8], lambda dr, dc, outer: halo_copy(-dr, -dc, outer).wait_recv())
     shift_row(1)
     shift_row(TR + 2)
     for i in range(1, TR + 3):
@@ -250,12 +250,6 @@
     s0[...] = pan[pl.ds(other_half, 768)].astype(bf16)
     g_sib = rcopy(s0, r0, send.at[8], srecv, sib)
     g_sib.start()
-    for cp in t_z:
-        cp.wait_recv()
-    for zz in range(2):
-        for b in range(2):
-            rows16 = jnp.concatenate([tz[q * 2 + zz][b * 4 : b * 4 + 4] for q in range(4)], axis=0)
-            tc[(zz * 2 + b) * 16 : (zz * 2 + b) * 16 + 16] = rows16.astype(bf16)
     g_sib.wait_recv()
     half = pan[pl.ds(own_half, 768)] + r0[...].astype(f32)
     s1[...] = half.astype(bf16)
@@ -269,12 +263,6 @@
         )
     for cp in g_xy:
         cp.start()
-    own_t = tb.at[core, pl.ds(pl.multiple_of(64 * xy, 64), 64)]
-    t_xy = [rcopy(tc, own_t, send.at[23 + j], txrecv.at[j], xyp(j)) for j in range(1, 16)]
-    for cp in t_xy:
-        cp.start()
-    tb[core, pl.ds(pl.multiple_of(64 * xy, 64), 64)] = tc[...]
-
     for h in range(1, 7):
         for s, (at, place) in enumerate((((h + 1) * TC, 0), ((h + 2) * TC - 16, 15))):
             put_row(feats, at, place, edge_f[8 * s + h : 8 * s + h + 1])
@@ -312,6 +300,18 @@
     feats[RING : RING + 32] = feat[2 * TC :].astype(bf16)
     deriv[RING : RING + 32] = slope[2 * TC :] * (side_on * row_on)
 
+    for cp in t_z:
+        cp.wait_recv()
+    for zz in range(2):
+        for b in range(2):
+            rows16 = jnp.concatenate([tz[q * 2 + zz][b * 4 : b * 4 + 4] for q in range(4)], axis=0)
+            tc[(zz * 2 + b) * 16 : (zz * 2 + b) * 16 + 16] = rows16.astype(bf16)
+    own_t = tb.at[core, pl.ds(pl.multiple_of(64 * xy, 64), 64)]
+    t_xy = [rcopy(tc, own_t, send.at[23 + j], txrecv.at[j], xyp(j)) for j in range(1, 16)]
+    for cp in t_xy:
+        cp.start()
+    tb[core, pl.ds(pl.multiple_of(64 * xy, 64), 64)] = tc[...]
+
     own48 = pl.multiple_of(own_half + 48 * xy, 16)
     acc = pan[pl.ds(own48, 48)]
     for j in range(1, 16):
@@ -322,10 +322,6 @@
     g_z = [rcopy(s2, r2.at[j], send.at[38 + j], zrecv.at[j], zp(j)) for j in range(1, 8)]
     for cp in g_z:
         cp.start()
-    for cp in t_xy:
-        cp.wait_recv()
-    t_fw = rcopy(tb.at[core], tb.at[core], send.at[46], tfrecv, sib)
-    t_fw.start()
     for a in range(3):
         for b in range(3):
             wt[a * CO : a * CO + CO, b * CI : b * CI + CI] = wv[3 * a + b].T
@@ -340,6 +336,10 @@
     for cp in g_ag:
         cp.start()
 
+    for cp in t_xy:
+        cp.wait_recv()
+    t_fw = rcopy(tb.at[core], tb.at[core], send.at[46], tfrecv, sib)
+    t_fw.start()
     t_fw.wait_recv()
 
     def tquad(i, k):
@@ -398,7 +398,6 @@
         for h in range(TR):
             edge[s, h] = total[h : h + 1]
 
-    outs = []
     for t in range(2):
         lhs = jnp.concatenate([gp[(4 * t + 2 - a) * TC : (4 * t + 6 - a) * TC] for a in range(3)], axis=1)
         total = jnp.dot(lhs, wt[...], preferred_element_type=f32)
@@ -408,19 +407,12 @@
             p0 = jnp.where(lane_row == TC - 1, edge[1, h], pltpu.roll(rows[:, 0:CI], TC - 1, axis=0))
             p2 = jnp.where(lane_row == 0, edge[0, h], pltpu.roll(rows[:, 2 * CI :], 1, axis=0))
             outv[h] = (rows[:, CI : 2 * CI] + p0 + p2).astype(bf16)
-        outs.append(pltpu.make_async_copy(outv.at[pl.ds(4 * t, 4)], grad_out.at[pl.ds(4 * t, 4)], osem.at[t]))
-        outs[t].start()
 
     own_row = zl * 256 + xy * 16 + zh * 4 + core * 2
     rows8 = gfull[pl.ds(pl.multiple_of((own_row // 8) * 8, 8), 8)]
     sub = lax.broadcasted_iota(jnp.int32, (8, CO), 0)
     for k in range(2):
         outg[k : k + 1] = jnp.sum(jnp.where(sub == own_row % 8 + k, rows8, 0.0), axis=0, keepdims=True)
-    g_out = pltpu.make_async_copy(outg, gram_out, osem.at[4])
-    g_out.start()
-    g_out.wait()
-    for cp in outs:
-        cp.wait()
     each_halo(kinds, lambda dr, dc, outer: halo_copy(dr, dc, outer).wait_send())
     for cp in [t_sib, g_sib, t_fw] + g_fw + t_z + g_xy + t_xy + g_z + g_ag:
         cp.wait_send()
@@ -429,8 +421,8 @@
 def finish(gram, grad, gram_out, grad_out, sem):
     one = pltpu.make_async_copy(gram, gram_out, sem.at[0])
     two = pltpu.make_async_copy(grad, grad_out, sem.at[1])
+    two.start()
     one.start()
-    two.start()
     one.wait()
     two.wait()
 
@@ -439,12 +431,13 @@
     hbm = pl.BlockSpec(memory_space=pl.ANY)
     vmem = pl.BlockSpec(memory_space=pltpu.VMEM)
     dma = pltpu.SemaphoreType.DMA
+    held = (pltpu.VMEM((2, CO), f32), pltpu.VMEM((TR, TC, CI), bf16))
     shapes = (jax.ShapeDtypeStruct((2, CO), f32), jax.ShapeDtypeStruct((TR, TC, CI), bf16))
     gram, grad = pl.pallas_call(
         kernel,
-        out_shape=shapes,
+        out_shape=held,
         in_specs=[hbm, hbm, vmem, hbm],
-        out_specs=(hbm, hbm),
+        out_specs=(vmem, vmem),
         scratch_shapes=[
             pltpu.VMEM((3, TR + 4, TC, CI), bf16),
             pltpu.VMEM((TR + 4, 8, CI), bf16),
@@ -472,8 +465,6 @@
             pltpu.VMEM((8, 8, 128), f32),
             pltpu.VMEM((64, 128), bf16),
             pltpu.VMEM((2, 1024, 128), bf16),
-            pltpu.VMEM((TR, TC, CI), bf16),
-            pltpu.VMEM((2, CO), f32),
             pltpu.VMEM((2, TR, 1, CI), f32),
             dma((3,)),
             dma((10,)),
@@ -488,15 +479,16 @@
             dma((8,)),
             dma((16,)),
             dma,
-            dma((5,)),
         ],
         compiler_params=pltpu.CompilerParams(
             collective_id=0, has_side_effects=True, vmem_limit_bytes=56 * 1024 * 1024
         ),
         name="style_grad",
     )(canvas, conv_weight.reshape(9, CI, CO), conv_bias, target_gram)
+    gram = pltpu.with_memory_space_constraint(gram, pltpu.VMEM)
+    grad = pltpu.with_memory_space_constraint(grad, pltpu.VMEM)
     return pl.pallas_call(
-        finish, out_shape=shapes, in_specs=[hbm, hbm], out_specs=(hbm, hbm), scratch_shapes=[dma((2,))], name="finish"
+        finish, out_shape=shapes, in_specs=[vmem, vmem], out_specs=(hbm, hbm), scratch_shapes=[dma((2,))], name="finish"
     )(gram, grad)
 
 

time: 63.4 us -> 44.8 us (0.71)
  Pallas kernels: 62.6 us -> 44 us
    pallas_call x2, Pallas kernels: 62.6 us -> 44 us  [the longest x1 43.2 us: on_device(): pl.pallas_call(kernel, out_shape=held, in_specs=[hbm, hbm, vmem, hbm], ou...]
where the time goes in v3:
time: 44.8 us; the launch traced here: 44.7 us
  Pallas kernels  44 us (98%)
  between operations  0.64 us (1%)
    pallas_call x1, Pallas kernels, on_device(): pl.pallas_call(kernel, out_shape=held, in_specs=[hbm, hbm, vmem, hbm], ou...  43.2 us

profile of v3, /device:TPU:1, one launch (start us, length us, event | category | flops | bytes accessed | tf_op | source)
XLA Modules:
  0.0 44.7 jit_solution(5400139637722823839)
XLA Ops:
  0.6 43.2 %style_grad.1 = (f32[2,512]{1,0:T(2,128)S(1)}, bf16[8,128,256]{2,1,0:T(8,128)(2,1)S(1)}) custom-call(bf16[8,128,256]{2,1,0:T(8,128)(2,1)} %canvas.1, bf16[9,256,512]{2,1,0:T(8,128)(2,1)} %bitcast.1, bf16[512]{0:T(512)(128)(2,1)} %bias.1, f32[2,512]{1,0:T(2,128)} %target.1), custom_call_target="tpu_custom_call" | custom-call | tf_op jit(solution)/shard_map/style_grad/pallas_call | solution.py:436
  43.9 0.8 %finish.1 = (f32[2,512]{1,0:T(2,128)}, bf16[8,128,256]{2,1,0:T(8,128)(2,1)}) custom-call(f32[2,512]{1,0:T(2,128)S(1)} %get-tuple-element.4.gram, bf16[8,128,256]{2,1,0:T(8,128)(2,1)S(1)} %get-tuple-element.5.grad), custom_call_target="tpu_custom_call" | custom-call | tf_op jit(solution)/shard_map/finish/pallas_call | solution.py:490

commit v4 on v3

--- a/solution.py
+++ b/solution.py
@@ -21,6 +21,12 @@
 Z_STEPS = (4, 3, 5, 2, 6, 1, 7)
 
 
+PANELS = ((0, 0, 128, 0), (0, 1, 256, 128), (1, 0, 256, 384), (1, 1, 256, 640), (2, 0, 128, 896), (2, 1, 256, 1024))
+GROWS = 1280
+HALF = GROWS // 2
+CHUNK = HALF // 16
+
+
 def gelu_pair(v):
     square = v * v
     half = 0.5 + 0.5 * jnp.tanh(v * (C0 + C1 * square))
@@ -31,9 +37,9 @@
 
 def kernel(
     canvas, weight, bias, target, outg, outv,
-    xs, left, right, wv, wt, feats, deriv, gp, gring, ringx, edgex, pan, s0, r0, s1, r1, s2, r2, gf,
+    xs, left, right, wv, wt, feats, deriv, gp, gring, ringx, edgex, pan, s0, r0, s1, r1, s2, r2, s3, gf,
     sym, tt, gfull, t2, tz, tc, tb, edge,
-    lsem, hsend, hrecv, send, xrecv, zrecv, arecv, frecv, srecv, tsrecv, tzrecv, txrecv, tfrecv,
+    lsem, hsend, hrecv, send, xrecv, zrecv, arecv, srecv, tsrecv, tzrecv, txrecv, tfrecv,
 ):
     r = lax.axis_index("rows")
     c = lax.axis_index("cols")
@@ -79,7 +85,7 @@
                     cond = this if cond is None else jnp.logical_and(cond, this)
             halo.append((dr, dc, cond))
     bar = pltpu.get_barrier_semaphore()
-    count = jnp.int32(23)
+    count = jnp.int32(38)
     for dr, dc, cond in halo:
         count = count + jnp.where(cond, 1, 0)
 
@@ -92,6 +98,10 @@
         pl.semaphore_signal(bar, inc=1, device_id=xyp(j), device_id_type=MESH)
     for j in range(1, 8):
         pl.semaphore_signal(bar, inc=1, device_id=zp(j), device_id_type=MESH)
+
+    for j in range(1, 16):
+        pl.semaphore_signal(bar, inc=1, device_id=(zl * 16 + xyk(j), c + 1 - 2 * core), device_id_type=MESH)
+
     pl.semaphore_wait(bar, count)
 
     kinds = [(dr, dc, 0) for dr, dc, _ in halo]
@@ -194,12 +204,13 @@
 
     def add_gram(feat, fresh):
         lo, hi = feat[:, 0:256], feat[:, 256:512]
-        for q, (one, two) in enumerate(((lo, lo), (lo, hi), (hi, hi))):
-            prod = lax.dot_general(one, two, (((0,), (0,)), ((), ())), preferred_element_type=f32)
-            for s in range(2):
-                at = (2 * q + s) * 256
-                part = prod[:, s * 128 : s * 128 + 128]
-                pan[at : at + 256] = part if fresh else pan[at : at + 256] + part
+        prods = [
+            lax.dot_general(one, two, (((0,), (0,)), ((), ())), preferred_element_type=f32)
+            for one, two in ((lo, lo), (lo, hi), (hi, hi))
+        ]
+        for q, side, rows, at in PANELS:
+            part = prods[q][0:rows, side * 128 : side * 128 + 128]
+            pan[at : at + rows] = part if fresh else pan[at : at + rows] + part
 
     feat, slope = gelu_pair(conv(taps(1, 6)))
     feats[2 * TC : 8 * TC] = feat.astype(bf16)
@@ -245,24 +256,24 @@
     corner = jnp.logical_or(sub16 % 8 == 0, sub16 % 8 == 7)
     add_gram(jnp.concatenate([feat[0 : 2 * TC], jnp.where(corner, 0.0, edge_f)], axis=0).astype(bf16), False)
 
-    own_half = pl.multiple_of(core * 768, 768)
-    other_half = pl.multiple_of((1 - core) * 768, 768)
-    s0[...] = pan[pl.ds(other_half, 768)].astype(bf16)
+    own_half = pl.multiple_of(core * HALF, HALF)
+    other_half = pl.multiple_of((1 - core) * HALF, HALF)
+    s0[...] = pan[pl.ds(other_half, HALF)].astype(bf16)
     g_sib = rcopy(s0, r0, send.at[8], srecv, sib)
     g_sib.start()
     g_sib.wait_recv()
-    half = pan[pl.ds(own_half, 768)] + r0[...].astype(f32)
-    s1[...] = half.astype(bf16)
-    pan[pl.ds(own_half, 768)] = half
-
-    g_xy = []
-    for j in range(1, 16):
-        k = xyk(j)
-        g_xy.append(
-            rcopy(s1.at[pl.ds(pl.multiple_of(48 * k, 16), 48)], r1.at[j], send.at[8 + j], xrecv.at[j], xyp(j))
-        )
+    both = pan[pl.ds(own_half, HALF)] + r0[...].astype(f32)
+    s1[...] = both.astype(bf16)
+
+    g_xy = [
+        rcopy(s1.at[pl.ds(pl.multiple_of(CHUNK * xyk(j), 8), CHUNK)], r1.at[j], send.at[8 + j], xrecv.at[j], xyp(j))
+        for j in range(1, 16)
+    ]
     for cp in g_xy:
         cp.start()
+    own_rows = pl.multiple_of(own_half + CHUNK * xy, 8)
+    pan[pl.ds(own_half, HALF)] = both
+
     for h in range(1, 7):
         for s, (at, place) in enumerate((((h + 1) * TC, 0), ((h + 2) * TC - 16, 15))):
             put_row(feats, at, place, edge_f[8 * s + h : 8 * s + h + 1])
@@ -312,8 +323,7 @@
         cp.start()
     tb[core, pl.ds(pl.multiple_of(64 * xy, 64), 64)] = tc[...]
 
-    own48 = pl.multiple_of(own_half + 48 * xy, 16)
-    acc = pan[pl.ds(own48, 48)]
+    acc = pan[pl.ds(own_rows, CHUNK)]
     for j in range(1, 16):
         g_xy[j - 1].wait_recv()
         acc = acc + r1[j].astype(f32)
@@ -329,16 +339,23 @@
     for j in range(1, 8):
         g_z[j - 1].wait_recv()
         acc = acc + r2[j].astype(f32)
-    gf[pl.ds(own48, 48)] = (acc * (1.0 / NPIX)).astype(bf16)
-
-    own_g = gf.at[pl.ds(own48, 48)]
-    g_ag = [rcopy(own_g, own_g, send.at[46 + j], arecv.at[j], xyp(j)) for j in range(1, 16)]
-    for cp in g_ag:
-        cp.start()
+    s3[...] = (acc * (1.0 / NPIX)).astype(bf16)
+
+    own_g = gf.at[pl.ds(own_rows, CHUNK)]
+    for other in (1, 0):
+        for j in range(1, 16):
+            cross = 16 * jnp.where(core == other, 0, 1)
+            dev = (zl * 16 + xyk(j), c - core + other)
+            rcopy(s3, own_g, send.at[79 + 16 * other + j], arecv.at[cross + j], dev).start()
+        if other == 1:
+            g_own = rcopy(s3, own_g, send.at[79], arecv.at[16], sib)
+            g_own.start()
+            keep = pltpu.make_async_copy(s3, own_g, lsem.at[0])
+            keep.start()
 
     for cp in t_xy:
         cp.wait_recv()
-    t_fw = rcopy(tb.at[core], tb.at[core], send.at[46], tfrecv, sib)
+    t_fw = rcopy(tb.at[core], tb.at[core], send.at[63], tfrecv, sib)
     t_fw.start()
     t_fw.wait_recv()
 
@@ -357,20 +374,22 @@
     tt[2] = t01.T
     tt[3] = t11 + t11.T
 
-    g_fw = [rcopy(own_g, own_g, send.at[62], frecv.at[0], sib)]
-    g_fw[0].start()
-    for j in range(15, 0, -1):
-        g_ag[j - 1].wait_recv()
-        got = gf.at[pl.ds(pl.multiple_of(own_half + 48 * xyk(j, -1), 16), 48)]
-        g_fw.append(rcopy(got, got, send.at[62 + j], frecv.at[j], sib))
-        g_fw[-1].start()
-    for cp in g_fw:
-        cp.wait_recv()
-
-    def gquad(q):
-        return jnp.concatenate([gf[q * 512 : q * 512 + 256], gf[q * 512 + 256 : q * 512 + 512]], axis=1).astype(f32)
-
-    g00, g01, g11 = gquad(0), gquad(1), gquad(2)
+    keep.wait()
+    for j in range(15, -1, -1):
+        for cross in (0, 1):
+            if j or cross:
+                rcopy(s3, own_g, send.at[79], arecv.at[16 * cross + j], sib).wait_recv()
+
+    def block(at):
+        return gf[at : at + 128].astype(f32)
+
+    def diagonal(at):
+        cross = block(at + 128)
+        top = jnp.concatenate([block(at), cross], axis=1)
+        return jnp.concatenate([top, jnp.concatenate([cross.T, block(at + 256)], axis=1)], axis=0)
+
+    g00, g11 = diagonal(0), diagonal(896)
+    g01 = jnp.concatenate([gf[384:640], gf[640:896]], axis=1).astype(f32)
     g10 = g01.T
     sym[0:256, 0:256] = (2.0 * g00 - tt[0]).astype(bf16)
     sym[0:256, 256:512] = (2.0 * g01 - tt[1]).astype(bf16)
@@ -414,8 +433,11 @@
     for k in range(2):
         outg[k : k + 1] = jnp.sum(jnp.where(sub == own_row % 8 + k, rows8, 0.0), axis=0, keepdims=True)
     each_halo(kinds, lambda dr, dc, outer: halo_copy(dr, dc, outer).wait_send())
-    for cp in [t_sib, g_sib, t_fw] + g_fw + t_z + g_xy + t_xy + g_z + g_ag:
+    for cp in [t_sib, g_sib, t_fw, g_own] + t_z + g_xy + t_xy + g_z:
         cp.wait_send()
+    for other in (1, 0):
+        for j in range(1, 16):
+            rcopy(s3, own_g, send.at[79 + 16 * other + j], arecv.at[j], sib).wait_send()
 
 
 def finish(gram, grad, gram_out, grad_out, sem):
@@ -450,14 +472,15 @@
             pltpu.VMEM((32, CO), f32),
             pltpu.VMEM((32, 9 * CI), f32),
             pltpu.VMEM((16, 9 * CI), f32),
-            pltpu.VMEM((1536, 128), f32),
-            pltpu.VMEM((768, 128), bf16),
-            pltpu.VMEM((768, 128), bf16),
-            pltpu.VMEM((768, 128), bf16),
-            pltpu.VMEM((16, 48, 128), bf16),
-            pltpu.VMEM((48, 128), bf16),
-            pltpu.VMEM((8, 48, 128), bf16),
-            pltpu.VMEM((1536, 128), bf16),
+            pltpu.VMEM((GROWS, 128), f32),
+            pltpu.VMEM((HALF, 128), bf16),
+            pltpu.VMEM((HALF, 128), bf16),
+            pltpu.VMEM((HALF, 128), bf16),
+            pltpu.VMEM((16, CHUNK, 128), bf16),
+            pltpu.VMEM((CHUNK, 128), bf16),
+            pltpu.VMEM((8, CHUNK, 128), bf16),
+            pltpu.VMEM((CHUNK, 128), bf16),
+            pltpu.VMEM((GROWS, 128), bf16),
             pltpu.VMEM((CO, CO), bf16),
             pltpu.VMEM((4, 256, 256), f32),
             pltpu.VMEM((CO, CO), f32),
@@ -469,11 +492,10 @@
             dma((3,)),
             dma((10,)),
             dma((10,)),
-            dma((78,)),
+            dma((112,)),
             dma((16,)),
             dma((8,)),
-            dma((16,)),
-            dma((16,)),
+            dma((32,)),
             dma,
             dma,
             dma((8,)),

time: 44.8 us -> 43.8 us (0.978)
  Pallas kernels: 44 us -> 43 us
    pallas_call x1, Pallas kernels: 43.2 us -> 42.2 us  [on_device(): pl.pallas_call(kernel, out_shape=held, in_specs=[hbm, hbm, vmem, hbm], ou...]
where the time goes in v4:
time: 43.8 us; the launch traced here: 43.7 us
  Pallas kernels  43 us (98%)
  between operations  0.64 us (1%)
    pallas_call x1, Pallas kernels, on_device(): pl.pallas_call(kernel, out_shape=held, in_specs=[hbm, hbm, vmem, hbm], ou...  42.2 us

profile of v4, /device:TPU:1, one launch (start us, length us, event | category | flops | bytes accessed | tf_op | source)
XLA Modules:
  0.0 43.7 jit_solution(10892917392248002480)
XLA Ops:
  0.6 42.2 %style_grad.1 = (f32[2,512]{1,0:T(2,128)S(1)}, bf16[8,128,256]{2,1,0:T(8,128)(2,1)S(1)}) custom-call(bf16[8,128,256]{2,1,0:T(8,128)(2,1)} %canvas.1, bf16[9,256,512]{2,1,0:T(8,128)(2,1)} %bitcast.1, bf16[512]{0:T(512)(128)(2,1)} %bias.1, f32[2,512]{1,0:T(2,128)} %target.1), custom_call_target="tpu_custom_call" | custom-call | tf_op jit(solution)/shard_map/style_grad/pallas_call | solution.py:458
  42.8 0.8 %finish.1 = (f32[2,512]{1,0:T(2,128)}, bf16[8,128,256]{2,1,0:T(8,128)(2,1)}) custom-call(f32[2,512]{1,0:T(2,128)S(1)} %get-tuple-element.4.gram, bf16[8,128,256]{2,1,0:T(8,128)(2,1)S(1)} %get-tuple-element.5.grad), custom_call_target="tpu_custom_call" | custom-call | tf_op jit(solution)/shard_map/finish/pallas_call | solution.py:512
